TPU v7x, 32 devices: a whole 2x2x4 slice. The times are simulated.
32 devices in a mesh: groups: 2 (over x), ctx: 16 (over z, y, core).
Axes of the slice: x: 2, y: 2, z: 4, core: 2. Of those that a mesh axis runs over, the one named last changes fastest.
Arguments:
- q_span: bfloat16 [2048, 8192], P(('groups', 'ctx')), parts along dimension 0, may hold values from -200 to 200
- k_span: bfloat16 [2048, 1024], P(('groups', 'ctx')), parts along dimension 0, may hold values from -30 to 30
- v_span: bfloat16 [2048, 1024], P(('groups', 'ctx')), parts along dimension 0, may hold values from -6 to 6
- k_prefix: bfloat16 [1024, 1024], P(('groups', 'ctx')), parts along dimension 0, may hold values from -30 to 30
- v_prefix: bfloat16 [1024, 1024], P(('groups', 'ctx')), parts along dimension 0, may hold values from -6 to 6
- start_offset: int32 [2], P('groups'), parts along dimension 0, may hold values from 0 to 511
- prefix_len: int32 [2], P('groups'), parts along dimension 0, may hold values from 1 to 512
- block_order: int32 [64], P('groups'), parts along dimension 0, may hold values from 0 to 31, each once
Outputs:
- attended: bfloat16 [2048, 8192], P(('groups', 'ctx')), parts along dimension 0
There are 2 independent parts, one for each index of `groups`. A program takes and returns all parts, laid end to end along the dimension named above; each array names one. Nothing has to cross between parts.
All inputs are finite; a program needn't handle non-finite values.
Results may differ from a plain program's by a relative error of at most 0.006.
Values may be sent and summed in bfloat16 or wider, within the bound.
No kernel may reach another device: no remote copies, remote signals or barrier semaphores. Data moves between devices by JAX's collectives and lax.ppermute only.
A program may use at most 128 MiB of HBM per device.

v0:
```python
import math

import jax
import jax.numpy as jnp
from jax import lax
from jax.sharding import PartitionSpec as P

HD = 128


NEG_FILL = -1e30


def local(q_span, k_span, v_span, k_prefix, v_prefix, start_offset, prefix_len, block_order):
    local_rows = q_span.shape[0]
    block_rows = local_rows // 2
    kv_heads = k_span.shape[1] // HD
    q_heads = q_span.shape[1] // HD
    table_len = block_order.shape[0]
    offset_value = start_offset[0]
    prefix_valid = prefix_len[0]
    scaling = 1.0 / math.sqrt(HD)
    members = lax.axis_size("ctx")
    heads_here = q_heads // members
    spread = members // kv_heads

    def widen(source):
        length = source.shape[0]
        grown = jnp.broadcast_to(
            source.reshape(length, kv_heads, 1, HD), (length, kv_heads, spread, HD)
        )
        return grown.reshape(length, members, HD)

    q_send = q_span.reshape(local_rows, members, heads_here * HD)
    q_whole, kc_whole, vc_whole, kp_whole, vp_whole = (
        lax.all_to_all(q_send, "ctx", split_axis=1, concat_axis=0, tiled=True),
        lax.all_to_all(widen(k_span), "ctx", split_axis=1, concat_axis=0, tiled=True),
        lax.all_to_all(widen(v_span), "ctx", split_axis=1, concat_axis=0, tiled=True),
        lax.all_to_all(widen(k_prefix), "ctx", split_axis=1, concat_axis=0, tiled=True),
        lax.all_to_all(widen(v_prefix), "ctx", split_axis=1, concat_axis=0, tiled=True),
    )
    whole_rows = q_whole.shape[0]
    prefix_whole = kp_whole.shape[0]
    key_stack = jnp.concatenate([kp_whole, kc_whole], 0).reshape(prefix_whole + whole_rows, HD)
    value_stack = jnp.concatenate([vp_whole, vc_whole], 0).reshape(prefix_whole + whole_rows, HD)
    row_index = jnp.arange(whole_rows, dtype=jnp.int32)
    which_block = row_index // block_rows
    matches = which_block[:, None] == jnp.arange(table_len, dtype=jnp.int32)[None, :]
    placed = jnp.sum(jnp.where(matches, block_order[None, :], 0), axis=1)
    all_pos = placed * block_rows + row_index % block_rows
    prefix_open = jnp.arange(prefix_whole, dtype=jnp.int32) < prefix_valid
    block_size = math.gcd(whole_rows, 512)
    block_count = whole_rows // block_size

    def head_block(packed):
        query_rows, query_place = packed
        scores = (
            jnp.einsum("qhd,kd->hqk", query_rows, key_stack, preferred_element_type=jnp.float32)
            * scaling
        )
        causal = (all_pos[None, :] <= query_place[:, None]) & (all_pos[None, :] >= offset_value)
        visible = jnp.concatenate(
            [jnp.broadcast_to(prefix_open[None, :], (block_size, prefix_whole)), causal], 1
        )
        scores = jnp.where(visible[None], scores, NEG_FILL)
        largest = jnp.max(scores, axis=-1, keepdims=True)
        weights = jnp.where(visible[None], jnp.exp(scores - largest), 0.0)
        denominator = jnp.sum(weights, axis=-1)
        summed = jnp.einsum(
            "hqk,kd->qhd",
            weights.astype(jnp.bfloat16),
            value_stack,
            preferred_element_type=jnp.float32,
        )
        result = summed / denominator.T[..., None]
        return result.reshape(block_size, heads_here * HD).astype(jnp.bfloat16)

    outputs = lax.map(
        head_block,
        (
            q_whole.reshape(block_count, block_size, heads_here, HD),
            all_pos.reshape(block_count, block_size),
        ),
    )
    outputs = outputs.reshape(whole_rows, 1, heads_here * HD)
    returned = lax.all_to_all(outputs, "ctx", split_axis=0, concat_axis=1, tiled=True)
    return returned.reshape(local_rows, q_heads * HD)


def solution(mesh):
    placed = (
        P(("groups", "ctx"), None),
        P(("groups", "ctx"), None),
        P(("groups", "ctx"), None),
        P(("groups", "ctx"), None),
        P(("groups", "ctx"), None),
        P("groups"),
        P("groups"),
        P("groups"),
    )
    return jax.shard_map(
        local, mesh=mesh, in_specs=placed, out_specs=P(("groups", "ctx"), None), check_vma=False
    )
```

profile of v0, /device:TPU:1, one launch (start us, length us, event | category | flops | bytes accessed | tf_op | source)
XLA Modules:
  0.0 155.2 jit_solution(3690061197051776769)
XLA Ops:
  0.0 0.9 copy_bitcast_fusion.10
  0.9 0.7 broadcast_in_dim.89
  1.6 7.3 %all-to-all-start.3 = ((bf16[32,16,128]{2,0,1:T(8,128)(2,1)}), bf16[32,16,128]{2,0,1:T(8,128)(2,1)S(1)}, u32[]{:S(2)}, u32[]{:S(2)}) async-start(bf16[32,16,128]{2,0,1:T(8,128)(2,1)} %bitcast.12), calls=%async_computation.3 | async-start | bytes 262144 | tf_op jit(solution)/shard_map/all_to_all | solution.py:40
  8.9 0.9 copy_bitcast_fusion.11
  9.8 5.9 %all-to-all-done.3 = bf16[32,16,128]{2,0,1:T(8,128)(2,1)S(1)} async-done(((bf16[32,16,128]{2,0,1:T(8,128)(2,1)}), bf16[32,16,128]{2,0,1:T(8,128)(2,1)S(1)}, u32[]{:S(2)}, u32[]{:S(2)}) %all-to-all-start.3) | async-done | bytes 131104 | tf_op jit(solution)/shard_map/all_to_all | solution.py:40
  15.7 0.7 broadcast_in_dim.85
  16.4 4.5 %all-to-all-start.1 = ((bf16[32,16,128]{2,0,1:T(8,128)(2,1)}), bf16[32,16,128]{2,0,1:T(8,128)(2,1)S(1)}, u32[]{:S(2)}, u32[]{:S(2)}) async-start(bf16[32,16,128]{2,0,1:T(8,128)(2,1)} %bitcast.3), calls=%async_computation.1 | async-start | bytes 262144 | tf_op jit(solution)/shard_map/all_to_all | solution.py:39
  20.9 6.8 %all-to-all-done.1 = bf16[32,16,128]{2,0,1:T(8,128)(2,1)S(1)} async-done(((bf16[32,16,128]{2,0,1:T(8,128)(2,1)}), bf16[32,16,128]{2,0,1:T(8,128)(2,1)S(1)}, u32[]{:S(2)}, u32[]{:S(2)}) %all-to-all-start.1) | async-done | bytes 131104 | tf_op jit(solution)/shard_map/all_to_all | solution.py:39
  27.8 0.8 broadcast_in_dim.91
  28.5 4.5 %all-to-all-start.4 = ((bf16[64,16,128]{2,0,1:T(8,128)(2,1)}), bf16[64,16,128]{2,0,1:T(8,128)(2,1)S(1)}, u32[]{:S(2)}, u32[]{:S(2)}) async-start(bf16[64,16,128]{2,0,1:T(8,128)(2,1)} %bitcast.16), calls=%async_computation.4 | async-start | bytes 524288 | tf_op jit(solution)/shard_map/all_to_all | solution.py:38
  33.1 0.9 copy_bitcast_fusion.9
  34.0 8.6 %all-to-all-done.4 = bf16[64,16,128]{2,0,1:T(8,128)(2,1)S(1)} async-done(((bf16[64,16,128]{2,0,1:T(8,128)(2,1)}), bf16[64,16,128]{2,0,1:T(8,128)(2,1)S(1)}, u32[]{:S(2)}, u32[]{:S(2)}) %all-to-all-start.4) | async-done | bytes 262176 | tf_op jit(solution)/shard_map/all_to_all | solution.py:38
  42.6 0.7 broadcast_in_dim.87
  43.4 3.9 %all-to-all-start.2 = ((bf16[64,16,128]{2,0,1:T(8,128)(2,1)}), bf16[64,16,128]{2,0,1:T(8,128)(2,1)S(1)}, u32[]{:S(2)}, u32[]{:S(2)}) async-start(bf16[64,16,128]{2,0,1:T(8,128)(2,1)} %bitcast.7), calls=%async_computation.2 | async-start | bytes 524288 | tf_op jit(solution)/shard_map/all_to_all | solution.py:37
  47.3 2.3 %copy.77 = bf16[8,16,8,512]{3,2,0,1:T(8,128)(2,1)} copy(bf16[8,16,8,512]{3,2,1,0:T(8,128)(2,1)} %bitcast.144) | data formatting | bytes 2097152 | tf_op jit(solution)/shard_map/reshape | solution.py:34
  49.6 7.3 %all-to-all-done.2 = bf16[64,16,128]{2,0,1:T(8,128)(2,1)S(1)} async-done(((bf16[64,16,128]{2,0,1:T(8,128)(2,1)}), bf16[64,16,128]{2,0,1:T(8,128)(2,1)S(1)}, u32[]{:S(2)}, u32[]{:S(2)}) %all-to-all-start.2) | async-done | bytes 262176 | tf_op jit(solution)/shard_map/all_to_all | solution.py:37
  56.9 4.1 %all-to-all-start = ((bf16[64,16,512]{2,0,1:T(8,128)(2,1)}), bf16[64,16,512]{2,0,1:T(8,128)(2,1)S(1)}, u32[]{:S(2)}, u32[]{:S(2)}) async-start(bf16[64,16,512]{2,0,1:T(8,128)(2,1)} %bitcast.119), calls=%async_computation | async-start | bytes 2097152 | tf_op jit(solution)/shard_map/all_to_all | solution.py:36
  61.2 0.9 copy.46
  62.1 0.8 maximum_bitcast_fusion
  62.9 21.3 %all-to-all-done = bf16[64,16,512]{2,0,1:T(8,128)(2,1)S(1)} async-done(((bf16[64,16,512]{2,0,1:T(8,128)(2,1)}), bf16[64,16,512]{2,0,1:T(8,128)(2,1)S(1)}, u32[]{:S(2)}, u32[]{:S(2)}) %all-to-all-start) | async-done | bytes 1048608 | tf_op jit(solution)/shard_map/all_to_all | solution.py:36
  84.5 34.0 %while.11 = (s32[]{:T(128)}, bf16[2,512,512]{2,1,0:T(8,128)(2,1)S(1)}, s32[1024]{0:T(1024)S(1)}, s32[2,512]{1,0:T(2,128)S(1)}, s32[]{:T(128)}, /*index=5*/bf16[2...) while((s32[]{:T(128)}, ...), condition=%wide.region_4.5_spmd.clone, body=%wide.region_1.4_spmd.clone.sunk | while | flops 1631849472 | bytes 20222080 | solution.py:78
  84.5 0.7 broadcast_compare_fusion.2
  85.6 0.7 iota_compare_fusion.3
  86.8 9.5 %fusion.60 = (f32[4,512]{1,0:T(4,128)S(1)}, bf16[4,512,1536]{2,1,0:T(8,128)(2,1)}) fusion(pred[512,1536]{1,0:T(8,128)(4,1)S(1)} %pad_add_fusion.2, bf16[1,512,4,128]{3,2,1,0:T(4,128)(2,1)S(1)} %constant_dynamic-slice_fusion.5, bf16[1536,128]{1,0:T(8,128)(2,1)} %get-tuple-element.221), kind=kOutput, calls=%fused_computation.58.clone.1 | convolution fusion | flops 824182272 | bytes 8003584 | tf_op jit(solution)/shard_map/while/body/eval_jaxpr/sub | solution.py:67
  96.3 5.0 %fusion.61 = bf16[512,4,128]{0,2,1:T(8,128)(2,1)S(1)} fusion(bf16[4,512,1536]{2,1,0:T(8,128)(2,1)} %get-tuple-element.191, f32[512,4]{0,1:T(4,128)S(1)} %bitcast.148, bf16[1536,128]{0,1:T(8,128)(2,1)} %get-tuple-element.222), kind=kOutput, calls=%fused_computation.18.clone.1 | convolution fusion | flops 805830656 | bytes 7217152 | tf_op jit(solution)/shard_map/while/body/eval_jaxpr/hqk,kd->qhd/dot_general | solution.py:69
  103.8 9.5 %fusion.60 = (f32[4,512]{1,0:T(4,128)S(1)}, bf16[4,512,1536]{2,1,0:T(8,128)(2,1)}) fusion(pred[512,1536]{1,0:T(8,128)(4,1)S(1)} %pad_add_fusion.2, bf16[1,512,4,128]{3,2,1,0:T(4,128)(2,1)S(1)} %constant_dynamic-slice_fusion.5, bf16[1536,128]{1,0:T(8,128)(2,1)} %get-tuple-element.221), kind=kOutput, calls=%fused_computation.58.clone.1 | convolution fusion | flops 824182272 | bytes 8003584 | tf_op jit(solution)/shard_map/while/body/eval_jaxpr/sub | solution.py:67
  113.3 5.0 %fusion.61 = bf16[512,4,128]{0,2,1:T(8,128)(2,1)S(1)} fusion(bf16[4,512,1536]{2,1,0:T(8,128)(2,1)} %get-tuple-element.191, f32[512,4]{0,1:T(4,128)S(1)} %bitcast.148, bf16[1536,128]{0,1:T(8,128)(2,1)} %get-tuple-element.222), kind=kOutput, calls=%fused_computation.18.clone.1 | convolution fusion | flops 805830656 | bytes 7217152 | tf_op jit(solution)/shard_map/while/body/eval_jaxpr/hqk,kd->qhd/dot_general | solution.py:69
  119.0 1.5 reduce
  120.5 0.8 reshape.95
  121.3 31.5 %all_to_all.102 = bf16[16,2,16384]{2,1,0:T(2,128)(2,1)S(1)} all-to-all(bf16[16,2,16384]{2,1,0:T(2,128)(2,1)S(1)} %reshape.95), channel_id=1, replica_groups=mesh['groups'=2,'ctx'=16] {'ctx'}, dimensions={0} | all-to-all | bytes 2097152 | tf_op jit(solution)/shard_map/all_to_all | solution.py:86
  152.8 1.0 reshape.96
  154.1 1.1 copy.59
  (31 shorter events, 5.0 us)
Async XLA Ops:
  0.0 20.9 %copy-start = (bf16[64,1024]{1,0:T(8,128)(2,1)S(1)}, bf16[64,1024]{1,0:T(8,128)(2,1)}, u32[]{:S(2)}) copy-start(bf16[64,1024]{1,0:T(8,128)(2,1)} %param.12) | copy-start | bytes 393220
  0.0 61.0 %copy-start.1 = (s32[32]{0:T(128)S(1)}, s32[32]{0:T(128)}, u32[]{:S(2)}) copy-start(s32[32]{0:T(128)} %param.17) | copy-start | bytes 388
  1.6 14.1 %all-to-all-start.3 = ((bf16[32,16,128]{2,0,1:T(8,128)(2,1)}), bf16[32,16,128]{2,0,1:T(8,128)(2,1)S(1)}, u32[]{:S(2)}, u32[]{:S(2)}) async-start(bf16[32,16,128]{2,0,1:T(8,128)(2,1)} %bitcast.12), calls=%async_computation.3 | async-start | bytes 262144 | tf_op jit(solution)/shard_map/all_to_all | solution.py:40
  16.4 11.4 %all-to-all-start.1 = ((bf16[32,16,128]{2,0,1:T(8,128)(2,1)}), bf16[32,16,128]{2,0,1:T(8,128)(2,1)S(1)}, u32[]{:S(2)}, u32[]{:S(2)}) async-start(bf16[32,16,128]{2,0,1:T(8,128)(2,1)} %bitcast.3), calls=%async_computation.1 | async-start | bytes 262144 | tf_op jit(solution)/shard_map/all_to_all | solution.py:39
  28.5 14.1 %all-to-all-start.4 = ((bf16[64,16,128]{2,0,1:T(8,128)(2,1)}), bf16[64,16,128]{2,0,1:T(8,128)(2,1)S(1)}, u32[]{:S(2)}, u32[]{:S(2)}) async-start(bf16[64,16,128]{2,0,1:T(8,128)(2,1)} %bitcast.16), calls=%async_computation.4 | async-start | bytes 524288 | tf_op jit(solution)/shard_map/all_to_all | solution.py:38
  43.4 13.5 %all-to-all-start.2 = ((bf16[64,16,128]{2,0,1:T(8,128)(2,1)}), bf16[64,16,128]{2,0,1:T(8,128)(2,1)S(1)}, u32[]{:S(2)}, u32[]{:S(2)}) async-start(bf16[64,16,128]{2,0,1:T(8,128)(2,1)} %bitcast.7), calls=%async_computation.2 | async-start | bytes 524288 | tf_op jit(solution)/shard_map/all_to_all | solution.py:37
  56.9 27.3 %all-to-all-start = ((bf16[64,16,512]{2,0,1:T(8,128)(2,1)}), bf16[64,16,512]{2,0,1:T(8,128)(2,1)S(1)}, u32[]{:S(2)}, u32[]{:S(2)}) async-start(bf16[64,16,512]{2,0,1:T(8,128)(2,1)} %bitcast.119), calls=%async_computation | async-start | bytes 2097152 | tf_op jit(solution)/shard_map/all_to_all | solution.py:36
where the time goes:
time: 156 us; the launch traced here: 155 us
  waiting for transfers between devices  50 us (32%)
  blocking collectives  31.5 us (20%)
  matrix products  28.8 us (18%)
  starting transfers between devices  24.4 us (16%)
  local copies, waits for them, and re-layouts  13.7 us (9%)
  other arithmetic  6.47 us (4%)
    all_to_all x1, blocking collectives, local(): lax.all_to_all(outputs, 'ctx', split_axis=0, concat_axis=1, tiled=True)  31.5 us
    all_to_all x1, waiting for transfers between devices, local(): lax.all_to_all(q_send, 'ctx', split_axis=1, concat_axis=0, tiled=True)  21.3 us
    sub x2, matrix products, head_block(): weights = jnp.where(visible[None], jnp.exp(scores - largest), 0.0)  18.9 us
    dot_general x2, matrix products, head_block(): jnp.einsum('hqk,kd->qhd', weights.astype(jnp.bfloat16), value_stack, pref...  9.91 us
    all_to_all x1, waiting for transfers between devices, local(): lax.all_to_all(widen(v_span), 'ctx', split_axis=1, concat_axis=0, tiled=T...  8.65 us
    all_to_all x1, starting transfers between devices, local(): lax.all_to_all(widen(v_prefix), 'ctx', split_axis=1, concat_axis=0, tiled...  7.34 us
    all_to_all x1, waiting for transfers between devices, local(): lax.all_to_all(widen(k_span), 'ctx', split_axis=1, concat_axis=0, tiled=T...  7.27 us
    all_to_all x1, waiting for transfers between devices, local(): lax.all_to_all(widen(k_prefix), 'ctx', split_axis=1, concat_axis=0, tiled...  6.84 us
  transfers between devices with their start and end apart: 5, of which 5 were waited for; matrix products, arithmetic and copies ran while one was open for 4% of the time, Pallas kernels for 0%

commit v1 on v0

v1 whole, which is shorter than its diff:
```python
import functools
import math

import jax
import jax.numpy as jnp
from jax import lax
from jax.experimental import pallas as pl
from jax.experimental.pallas import tpu as pltpu
from jax.sharding import PartitionSpec as P

HD = 128
MASKED = -1e30
NEVER = 1 << 30


def chip_ring(mesh):
    names = list(mesh.axis_names)
    line = mesh.devices.transpose([names.index("ctx")] + [i for i, n in enumerate(names) if n != "ctx"])
    line = line.reshape(line.shape[0], -1)[::2, 0]
    natural = list(range(len(line)))
    if not all(hasattr(d, "coords") for d in line):
        return natural
    coords = [tuple(d.coords) for d in line]
    axes = [a for a in range(len(coords[0])) if len({c[a] for c in coords}) > 1]
    if len(axes) == 2:
        for narrow, wide in (axes, axes[::-1]):
            columns = sorted({c[narrow] for c in coords})
            if len(columns) == 2:
                up = sorted((i for i in natural if coords[i][narrow] == columns[0]), key=lambda i: coords[i][wide])
                down = sorted((i for i in natural if coords[i][narrow] == columns[1]), key=lambda i: -coords[i][wide])
                return up + down
    return natural


def attend_kernel(n_pieces, span_rows, first, last, coef, c_ref, *refs):
    q_mine, q_other, kpos, qpos = refs[:4]
    pieces = refs[4 : 4 + n_pieces]
    rest = refs[4 + n_pieces :]
    if not first:
        m_in, l_in, a_in = rest[:3]
        rest = rest[3:]
    if last:
        out_mine, out_other, bias = rest
    else:
        m_out, l_out, a_out, bias = rest
    rows = q_mine.shape[0]
    heads = q_mine.shape[1] // HD
    keys_piece = pieces[0].shape[0] // 2

    @pl.when(pl.program_id(0) == 0)
    def _():
        bias[...] = jnp.where(kpos[...] <= qpos[...], 0.0, MASKED)

    k = jnp.concatenate([p[:keys_piece, :] for p in pieces], axis=0)
    v = jnp.concatenate([p[keys_piece:, :] for p in pieces], axis=0)
    v = jnp.concatenate([v, jnp.ones_like(v)], axis=1)
    for h in range(heads):
        at = slice(h * HD, (h + 1) * HD)
        block = slice(h * 2 * rows, (h + 1) * 2 * rows)
        q = jnp.concatenate([q_mine[:, at], q_other[:, at]], axis=0)
        s = lax.dot_general(q, k, (((1,), (1,)), ((), ())), preferred_element_type=jnp.float32)
        s = s + bias[...]
        m = jnp.max(s, axis=1, keepdims=True)
        if not first:
            m_old = m_in[block, :]
            m_wide = jnp.maximum(m_old, m)
            m = m_wide[:, :1]
            scale = jnp.exp2((m_old - m_wide) * coef)
        w = jnp.exp2((s - m) * coef).astype(jnp.bfloat16)
        pv = jnp.dot(w, v, preferred_element_type=jnp.float32)
        acc, total = pv[:, :HD], pv[:, HD:]
        if not first:
            acc = acc + a_in[block, :] * scale
            total = total + l_in[block, :] * scale
        if last:
            o = (acc / total).astype(jnp.bfloat16)
            out_mine[:, at] = o[:rows]
            out_other[:, at] = o[rows:]
        else:
            m_out[block, :] = jnp.broadcast_to(m, (2 * rows, HD)) if first else m_wide
            l_out[block, :] = total
            a_out[block, :] = acc


def attend(core, q_mine, q_other, kpos, qpos, pieces, state, last, coef):
    rows, q_half = q_other.shape
    heads_here = pieces[0].shape[1] // HD
    width = q_half // heads_here
    keys = kpos.shape[1]
    first = state is None
    q_rows = 2 * rows * (width // HD)
    piece_rows = pieces[0].shape[0]
    state_spec = pl.BlockSpec((q_rows, HD), lambda g, c: (g, 0))
    in_specs = [
        pl.BlockSpec((rows, width), lambda g, c: (0, c[0] * heads_here + g)),
        pl.BlockSpec((rows, width), lambda g, c: (0, g)),
        pl.BlockSpec((1, keys), lambda g, c: (0, 0)),
        pl.BlockSpec((2 * rows, 1), lambda g, c: (0, 0)),
    ] + [pl.BlockSpec((piece_rows, HD), lambda g, c: (0, g))] * len(pieces)
    args = [core, q_mine, q_other, kpos, qpos, *pieces]
    aliases = {}
    if not first:
        if not last:
            aliases = {len(args) + i: i for i in range(3)}
        args += list(state)
        in_specs += [state_spec] * 3
    if last:
        out_shape = (
            jax.ShapeDtypeStruct(q_mine.shape, jnp.bfloat16),
            jax.ShapeDtypeStruct(q_other.shape, jnp.bfloat16),
        )
        out_specs = (
            pl.BlockSpec((rows, width), lambda g, c: (0, c[0] * heads_here + g)),
            pl.BlockSpec((rows, width), lambda g, c: (0, g)),
        )
    else:
        out_shape = (jax.ShapeDtypeStruct((q_rows * heads_here, HD), jnp.float32),) * 3
        out_specs = (state_spec,) * 3
    total_rows = q_rows * heads_here
    return pl.pallas_call(
        functools.partial(attend_kernel, len(pieces), rows, first, last, coef),
        grid_spec=pltpu.PrefetchScalarGridSpec(
            num_scalar_prefetch=1,
            grid=(heads_here,),
            in_specs=in_specs,
            out_specs=out_specs,
            scratch_shapes=[pltpu.VMEM((2 * rows, keys), jnp.float32)],
        ),
        out_shape=out_shape,
        input_output_aliases=aliases,
        compiler_params=pltpu.CompilerParams(vmem_limit_bytes=24 << 20),
        cost_estimate=pl.CostEstimate(
            flops=4 * total_rows * keys * HD,
            bytes_accessed=4 * total_rows * HD * 4,
            transcendentals=total_rows * keys,
        ),
    )(*args)


def place_kernel(c_ref, got, whole, out):
    out[...] = got[...]


def place(core, got, whole):
    rows, width = got.shape
    return pl.pallas_call(
        place_kernel,
        grid_spec=pltpu.PrefetchScalarGridSpec(
            num_scalar_prefetch=1,
            grid=(1,),
            in_specs=[
                pl.BlockSpec((rows, width), lambda g, c: (0, 0)),
                pl.BlockSpec(memory_space=pl.ANY),
            ],
            out_specs=pl.BlockSpec((rows, width), lambda g, c: (0, 1 - c[0])),
        ),
        out_shape=jax.ShapeDtypeStruct(whole.shape, whole.dtype),
        input_output_aliases={2: 0},
        compiler_params=pltpu.CompilerParams(vmem_limit_bytes=8 << 20),
    )(core, got, whole)


def make_local(ring):
    chips = len(ring)
    place_of = {chip: i for i, chip in enumerate(ring)}

    def pairs(shift, cross):
        return [
            (2 * chip + c, 2 * ring[(place_of[chip] + shift) % chips] + (c ^ cross))
            for chip in range(chips)
            for c in range(2)
        ]

    def send(x, shift, cross=0):
        return lax.ppermute(x, "ctx", pairs(shift, cross))

    shifts = [0] + [s for step in range(1, chips // 2) for s in (step, -step)] + [chips // 2]
    arrivals = [
        [2 * ring[(place_of[d // 2] - s) % chips] + (d % 2 ^ cross) for s in shifts for cross in (0, 1)]
        for d in range(2 * chips)
    ]

    def local(q_span, k_span, v_span, k_prefix, v_prefix, start_offset, prefix_len, block_order):
        rows, q_width = q_span.shape
        block = rows // 2
        prefix_rows = k_prefix.shape[0]
        kv_width = k_span.shape[1]
        members = 2 * chips
        me = lax.axis_index("ctx")
        core = me % 2
        coef = 1.0 / math.sqrt(HD) * math.log2(math.e)

        kv = jnp.concatenate([k_span, k_prefix, v_span, v_prefix], axis=0)
        mine = lax.dynamic_slice_in_dim(kv, core * (kv_width // 2), kv_width // 2, 1)
        theirs = lax.dynamic_slice_in_dim(kv, (1 - core) * (kv_width // 2), kv_width // 2, 1)
        q_theirs = lax.dynamic_slice_in_dim(q_span, (1 - core) * (q_width // 2), q_width // 2, 1)

        span_pos = jnp.repeat(block_order.reshape(members, 2), block, axis=1) * block + jnp.tile(
            jnp.arange(block, dtype=jnp.int32), 2
        )
        span_key = jnp.where(span_pos >= start_offset[0], span_pos, NEVER)
        prefix_id = jnp.arange(members * prefix_rows, dtype=jnp.int32).reshape(members, prefix_rows)
        prefix_key = jnp.where(prefix_id < prefix_len[0], -1, NEVER)
        key_pos = jnp.concatenate([span_key, prefix_key], axis=1)
        order = jnp.asarray(arrivals, jnp.int32)[me]
        picked = order[:, None] == jnp.arange(members, dtype=jnp.int32)[None, :]
        key_pos = jnp.sum(jnp.where(picked[:, :, None], key_pos[None], 0), axis=1)
        query_pos = jnp.sum(jnp.where(picked[:2, :, None], span_pos[None], 0), axis=1).reshape(2 * rows, 1)
        core_arr = core.astype(jnp.int32).reshape(1)

        own = [mine, send(theirs, 0, 1)]
        q_other = send(q_theirs, 0, 1)
        ahead = [send(mine, 1), send(theirs, 1, 1)]
        behind = [send(mine, -1), send(theirs, -1, 1)]
        groups = [own + ahead + behind]
        for _ in range(chips // 2 - 2):
            ahead = [send(x, 1) for x in ahead]
            behind = [send(x, -1) for x in behind]
            groups.append(ahead + behind)
        groups.append([send(ahead[0], 1), send(behind[1], -1)])

        state = None
        at = 0
        for i, pieces in enumerate(groups):
            n = len(pieces)
            kpos = key_pos[at : at + n].reshape(1, -1)
            at += n
            last = i == len(groups) - 1
            state = attend(core_arr, q_span, q_other, kpos, query_pos, pieces, state, last, coef)
        out, out_theirs = state
        return place(core_arr, send(out_theirs, 0, 1), out)

    return local


def solution(mesh):
    split = P(("groups", "ctx"), None)
    placed = (split,) * 5 + (P("groups"),) * 3
    return jax.shard_map(
        make_local(chip_ring(mesh)), mesh=mesh, in_specs=placed, out_specs=split, check_vma=False
    )
```

time: 156 us -> 73.4 us (0.47)
  waiting for transfers between devices: 50 us -> 7.48 us
  Pallas kernels: 0 us -> 33.7 us
  blocking collectives: 31.5 us -> 0 us
  matrix products: 28.8 us -> 0 us
  starting transfers between devices: 24.4 us -> 15.4 us
  other arithmetic: 6.47 us -> 1.02 us
    all_to_all x5 -> x0, waiting for transfers between devices: 50 us -> none  [the longest x1 21.3 us: local(): lax.all_to_all(q_send, 'ctx', split_axis=1, concat_axis=0, tiled=True)]
    pallas_call x0 -> x5, Pallas kernels: none -> 33.7 us  [the longest x4 32.9 us: attend(): pl.pallas_call(functools.partial(attend_kernel, len(pieces), rows, first,...]
    all_to_all x1 -> x0, blocking collectives: 31.5 us -> none  [local(): lax.all_to_all(outputs, 'ctx', split_axis=0, concat_axis=1, tiled=True)]
    all_to_all x5 -> x0, starting transfers between devices: 24.4 us -> none  [the longest x1 7.34 us: local(): lax.all_to_all(widen(v_prefix), 'ctx', split_axis=1, concat_axis=0, tiled...]
    sub x2 -> x0, matrix products: 18.9 us -> none  [head_block(): weights = jnp.where(visible[None], jnp.exp(scores - largest), 0.0)]
    ppermute x0 -> x17, starting transfers between devices: none -> 15.4 us  [send(): return lax.ppermute(x, 'ctx', pairs(shift, cross))]
    dot_general x2 -> x0, matrix products: 9.91 us -> none  [head_block(): jnp.einsum('hqk,kd->qhd', weights.astype(jnp.bfloat16), value_stack, pref...]
    ppermute x0 -> x17, waiting for transfers between devices: none -> 7.48 us  [send(): return lax.ppermute(x, 'ctx', pairs(shift, cross))]
  transfers between devices with their start and end apart: 5 -> 17, of which waited for: 5 -> 7; matrix products, arithmetic and copies ran while one was open for 4% -> 6% of each run, Pallas kernels for 0% -> 28%
where the time goes in v1:
time: 73.4 us; the launch traced here: 72.5 us
  Pallas kernels  33.7 us (46%)
  starting transfers between devices  15.4 us (21%)
  local copies, waits for them, and re-layouts  13.4 us (18%)
  waiting for transfers between devices  7.48 us (10%)
  between operations  1.46 us (2%)
  other arithmetic  1.02 us (1%)
    pallas_call x4, Pallas kernels, attend(): pl.pallas_call(functools.partial(attend_kernel, len(pieces), rows, first,...  32.9 us
    ppermute x17, starting transfers between devices, send(): return lax.ppermute(x, 'ctx', pairs(shift, cross))  15.4 us
    unnamed x21, local copies, waits for them, and re-layouts  9.17 us
    ppermute x17, waiting for transfers between devices, send(): return lax.ppermute(x, 'ctx', pairs(shift, cross))  7.48 us
    dynamic_slice x1, local copies, waits for them, and re-layouts, local(): lax.dynamic_slice_in_dim(q_span, (1 - core) * (q_width // 2), q_width //...  1.87 us
  transfers between devices with their start and end apart: 17, of which 7 were waited for; matrix products, arithmetic and copies ran while one was open for 6% of the time, Pallas kernels for 28%

profile of v1, /device:TPU:1, one launch (start us, length us, event | category | flops | bytes accessed | tf_op | source)
XLA Modules:
  0.0 72.5 jit_solution(12912222618708436852)
XLA Ops:
  0.0 1.0 %constant_dynamic-update-slice_fusion.3 = bf16[192,1024]{1,0:T(8,128)(2,1)S(1)} fusion(bf16[64,1024]{1,0:T(8,128)(2,1)} %param.10), kind=kLoop, calls=%fused_computation.6 | loop fusion | bytes 262144
  1.0 0.8 %constant_dynamic-update-slice_fusion.2 = bf16[192,1024]{1,0:T(8,128)(2,1)S(1)} fusion(bf16[192,1024]{1,0:T(8,128)(2,1)S(1)} %constant_dynamic-update-slice_fusion.3, bf16[32,1024]{1,0:T(8,128)(2,1)} %param.12), kind=kLoop, calls=%fused_computation.5 | loop fusion | bytes 131072
  1.9 0.9 %constant_dynamic-update-slice_fusion.1 = bf16[192,1024]{1,0:T(8,128)(2,1)S(1)} fusion(bf16[192,1024]{1,0:T(8,128)(2,1)S(1)} %constant_dynamic-update-slice_fusion.2, bf16[64,1024]{1,0:T(8,128)(2,1)} %param.11), kind=kLoop, calls=%fused_computation.4 | loop fusion | bytes 262144
  2.8 0.8 %constant_dynamic-update-slice_fusion = bf16[192,1024]{1,0:T(8,128)(2,1)S(1)} fusion(bf16[192,1024]{1,0:T(8,128)(2,1)S(1)} %constant_dynamic-update-slice_fusion.1, bf16[32,1024]{1,0:T(8,128)(2,1)} %param.13), kind=kLoop, calls=%fused_computation.3 | loop fusion | bytes 131072 | tf_op jit(solution)/shard_map/concatenate | solution.py:193
  3.7 2.2 %collective-permute-start.1 = (bf16[192,512]{1,0:T(8,128)(2,1)S(1)}, bf16[192,512]{1,0:T(8,128)(2,1)S(1)}, u32[]{:S(2)}, u32[]{:S(2)}) collective-permute-start(bf16[192,512]{1,0:T(8,128)(2,1)S(1)} %get-tuple-element.30.refs_4_), channel_id=1, source_target_pairs={{0,4},{1,5},{2,0},{3,1},{4,8},{5,9},{6,2},{7,3},{8,12},{9,13},{10,... | collective-permute-start | bytes 589832 | tf_op jit(solution)/shard_map/ppermute | solution.py:175
  5.8 1.0 %collective-permute-start.15 = (bf16[192,512]{1,0:T(8,128)(2,1)S(1)}, bf16[192,512]{1,0:T(8,128)(2,1)S(1)}, u32[]{:S(2)}, u32[]{:S(2)}) collective-permute-start(bf16[192,512]{1,0:T(8,128)(2,1)S(1)} %get-tuple-element.29), channel_id=1, source_target_pairs={{0,1},{1,0},{2,3},{3,2},{4,5},{5,4},{6,7},{7,6},{8,9},{9,8},{10,11... | collective-permute-start | bytes 589832 | tf_op jit(solution)/shard_map/ppermute | solution.py:175
  6.8 1.6 %collective-permute-start.5 = (bf16[192,512]{1,0:T(8,128)(2,1)S(1)}, bf16[192,512]{1,0:T(8,128)(2,1)S(1)}, u32[]{:S(2)}, u32[]{:S(2)}) collective-permute-start(bf16[192,512]{1,0:T(8,128)(2,1)S(1)} %get-tuple-element.29), channel_id=1, source_target_pairs={{0,3},{1,2},{2,7},{3,6},{4,1},{5,0},{6,11},{7,10},{8,5},{9,4},{10,... | collective-permute-start | bytes 589832 | tf_op jit(solution)/shard_map/ppermute | solution.py:175
  10.9 1.9 %constant_dynamic-slice_fusion.3 = bf16[64,4096]{1,0:T(8,128)(2,1)} fusion(bf16[64,8192]{1,0:T(8,128)(2,1)} %refs_0_.7, s32[]{:T(128)S(6)} %select_n.36), kind=kLoop, calls=%fused_computation.15 | loop fusion | bytes 1048580 | tf_op jit(solution)/shard_map/dynamic_slice | solution.py:196
  12.7 0.7 fusion.1
  13.9 1.4 %collective-permute-start.2 = (bf16[192,512]{1,0:T(8,128)(2,1)S(1)}, bf16[192,512]{1,0:T(8,128)(2,1)S(1)}, u32[]{:S(2)}, u32[]{:S(2)}) collective-permute-start(bf16[192,512]{1,0:T(8,128)(2,1)S(1)} %collective-permute-done.1.refs_6_), channel_id=1, source_target_pairs={{0,4},{1,5},{2,0},{3,1},{4,8},{5,9},{6,2},{7,3},{8,12},{9,13},{10,... | collective-permute-start | bytes 589832 | tf_op jit(solution)/shard_map/ppermute | solution.py:175
  15.4 0.7 copy-done.1
  16.9 0.7 copy-done.7
  17.8 1.3 %collective-permute-start.10 = (bf16[192,512]{1,0:T(8,128)(2,1)}, bf16[192,512]{1,0:T(8,128)(2,1)S(1)}, u32[]{:S(2)}, u32[]{:S(2)}) collective-permute-start(bf16[192,512]{1,0:T(8,128)(2,1)} %collective-permute-done.9.refs_7_), channel_id=1, source_target_pairs={{0,4},{1,5},{2,0},{3,1},{4,8},{5,9},{6,2},{7,3},{8,12},{9,13},{10,... | collective-permute-start | bytes 589832 | tf_op jit(solution)/shard_map/ppermute | solution.py:175
  19.1 0.7 copy-done.5
  20.6 1.2 %collective-permute-start.3 = (bf16[192,512]{1,0:T(8,128)(2,1)S(1)}, bf16[192,512]{1,0:T(8,128)(2,1)S(1)}, u32[]{:S(2)}, u32[]{:S(2)}) collective-permute-start(bf16[192,512]{1,0:T(8,128)(2,1)S(1)} %collective-permute-done.2.refs_4_), channel_id=1, source_target_pairs={{0,4},{1,5},{2,0},{3,1},{4,8},{5,9},{6,2},{7,3},{8,12},{9,13},{10,... | collective-permute-start | bytes 589832 | tf_op jit(solution)/shard_map/ppermute | solution.py:175
  21.9 1.1 %collective-permute-done.6.refs_7_ = bf16[192,512]{1,0:T(8,128)(2,1)S(1)} collective-permute-done((bf16[192,512]{1,0:T(8,128)(2,1)S(1)}, bf16[192,512]{1,0:T(8,128)(2,1)S(1)}, u32[]{:S(2)}, u32[]{:S(2)}) %collective-permute-start.6) | collective-permute-done | bytes 196640 | tf_op jit(solution)/shard_map/ppermute | solution.py:175
  23.3 1.1 %collective-permute-done.10.refs_5_ = bf16[192,512]{1,0:T(8,128)(2,1)S(1)} collective-permute-done((bf16[192,512]{1,0:T(8,128)(2,1)}, bf16[192,512]{1,0:T(8,128)(2,1)S(1)}, u32[]{:S(2)}, u32[]{:S(2)}) %collective-permute-start.10) | collective-permute-done | bytes 196640 | tf_op jit(solution)/shard_map/ppermute | solution.py:175
  24.4 1.5 %collective-permute-start.11 = (bf16[192,512]{1,0:T(8,128)(2,1)S(1)}, bf16[192,512]{1,0:T(8,128)(2,1)S(1)}, u32[]{:S(2)}, u32[]{:S(2)}) collective-permute-start(bf16[192,512]{1,0:T(8,128)(2,1)S(1)} %collective-permute-done.10.refs_5_), channel_id=1, source_target_pairs={{0,4},{1,5},{2,0},{3,1},{4,8},{5,9},{6,2},{7,3},{8,12},{9,13},{10,... | collective-permute-start | bytes 589832 | tf_op jit(solution)/shard_map/ppermute | solution.py:175
  25.9 1.3 %collective-permute-done.13.refs_6_ = bf16[192,512]{1,0:T(8,128)(2,1)S(1)} collective-permute-done((bf16[192,512]{1,0:T(8,128)(2,1)S(1)}, bf16[192,512]{1,0:T(8,128)(2,1)S(1)}, u32[]{:S(2)}, u32[]{:S(2)}) %collective-permute-start.13) | collective-permute-done | bytes 196640 | tf_op jit(solution)/shard_map/ppermute | solution.py:175
  28.6 1.5 %collective-permute-start.4 = (bf16[192,512]{1,0:T(8,128)(2,1)S(1)}, bf16[192,512]{1,0:T(8,128)(2,1)S(1)}, u32[]{:S(2)}, u32[]{:S(2)}) collective-permute-start(bf16[192,512]{1,0:T(8,128)(2,1)S(1)} %collective-permute-done.3.refs_4_), channel_id=1, source_target_pairs={{0,4},{1,5},{2,0},{3,1},{4,8},{5,9},{6,2},{7,3},{8,12},{9,13},{10,... | collective-permute-start | bytes 589832 | tf_op jit(solution)/shard_map/ppermute | solution.py:175
  30.1 1.3 %collective-permute-done.7.refs_7_ = bf16[192,512]{1,0:T(8,128)(2,1)S(1)} collective-permute-done((bf16[192,512]{1,0:T(8,128)(2,1)S(1)}, bf16[192,512]{1,0:T(8,128)(2,1)S(1)}, u32[]{:S(2)}, u32[]{:S(2)}) %collective-permute-start.7) | collective-permute-done | bytes 196640 | tf_op jit(solution)/shard_map/ppermute | solution.py:175
  31.7 0.9 %copy-done.2 = bf16[192,512]{1,0:T(8,128)(2,1)S(1)} copy-done((bf16[192,512]{1,0:T(8,128)(2,1)S(1)}, bf16[192,512]{1,0:T(8,128)(2,1)}, u32[]{:S(2)}) %copy-start.2) | copy-done | bytes 196632
  32.6 0.9 %copy-done.4 = bf16[192,512]{1,0:T(8,128)(2,1)S(1)} copy-done((bf16[192,512]{1,0:T(8,128)(2,1)S(1)}, bf16[192,512]{1,0:T(8,128)(2,1)}, u32[]{:S(2)}) %copy-start.4) | copy-done | bytes 196632
  33.5 0.9 %copy-done.6 = bf16[192,512]{1,0:T(8,128)(2,1)S(1)} copy-done((bf16[192,512]{1,0:T(8,128)(2,1)S(1)}, bf16[192,512]{1,0:T(8,128)(2,1)}, u32[]{:S(2)}) %copy-start.6) | copy-done | bytes 196632
  34.5 0.9 %copy-done.8 = bf16[192,512]{1,0:T(8,128)(2,1)S(1)} copy-done((bf16[192,512]{1,0:T(8,128)(2,1)S(1)}, bf16[192,512]{1,0:T(8,128)(2,1)}, u32[]{:S(2)}) %copy-start.8) | copy-done | bytes 196632
  35.4 6.9 %shard_map.91 = (f32[4096,128]{1,0:T(8,128)S(1)}, f32[4096,128]{1,0:T(8,128)S(1)}, f32[4096,128]{1,0:T(8,128)S(1)}) custom-call(s32[1]{0:T(128)} %bitcast.c_ref, bf16[64,8192]{1,0:T(8,128)(2,1)S(1)} %copy-done, bf16[64,4096]{1,0:T(8,128)(2,1)S(1)} %collective-permute-done.refs_1_, s32[1,576]{1,0:T(1,128)S(1)} %reshape.89.refs_2_, ...), custom_call_target="tpu_custom_call" | custom-call | flops 1207959552 | bytes 8388608 | tf_op jit(solution)/shard_map/pallas_call | solution.py:120
  42.3 6.9 %shard_map.92 = (f32[4096,128]{1,0:T(8,128)S(1)}, f32[4096,128]{1,0:T(8,128)S(1)}, f32[4096,128]{1,0:T(8,128)S(1)}) custom-call(s32[1]{0:T(128)} %bitcast.c_ref, bf16[64,8192]{1,0:T(8,128)(2,1)S(1)} %copy-done, bf16[64,4096]{1,0:T(8,128)(2,1)S(1)} %collective-permute-done.refs_1_, ...), custom_call_target="tpu_custom_call", output_to_operand_aliasing={{0}: (9, {}), {1}: (10, {}), {2}: (11, {})} | custom-call | flops 805306368 | bytes 8388608 | tf_op jit(solution)/shard_map/pallas_call | solution.py:120
  49.2 6.9 %shard_map.93 = (f32[4096,128]{1,0:T(8,128)S(1)}, f32[4096,128]{1,0:T(8,128)S(1)}, f32[4096,128]{1,0:T(8,128)S(1)}) custom-call(s32[1]{0:T(128)} %bitcast.c_ref, bf16[64,8192]{1,0:T(8,128)(2,1)S(1)} %copy-done, bf16[64,4096]{1,0:T(8,128)(2,1)S(1)} %collective-permute-done.refs_1_, ...), custom_call_target="tpu_custom_call", output_to_operand_aliasing={{0}: (9, {}), {1}: (10, {}), {2}: (11, {})} | custom-call | flops 805306368 | bytes 8388608 | tf_op jit(solution)/shard_map/pallas_call | solution.py:120
  56.1 12.2 %shard_map.94 = (bf16[64,8192]{1,0:T(8,128)(2,1)}, bf16[64,4096]{1,0:T(8,128)(2,1)S(1)}) custom-call(s32[1]{0:T(128)} %bitcast.c_ref, bf16[64,8192]{1,0:T(8,128)(2,1)S(1)} %copy-done, bf16[64,4096]{1,0:T(8,128)(2,1)S(1)} %collective-permute-done.refs_1_, s32[1,192]{1,0:T(1,128)S(1)} %reshape.85.refs_2_, s32[128,1]{1,0:T(8,128)S(1)} %reshape.90.refs_3_, ...), custom_call_target="tpu_custom_call" | custom-call | flops 402653184 | bytes 8388608 | tf_op jit(solution)/shard_map/pallas_call | solution.py:120
  68.4 1.8 %collective-permute-start.16 = (bf16[64,4096]{1,0:T(8,128)(2,1)S(1)}, bf16[64,4096]{1,0:T(8,128)(2,1)S(1)}, u32[]{:S(2)}, u32[]{:S(2)}) collective-permute-start(bf16[64,4096]{1,0:T(8,128)(2,1)S(1)} %get-tuple-element.25), channel_id=1, source_target_pairs={{0,1},{1,0},{2,3},{3,2},{4,5},{5,4},{6,7},{7,6},{8,9},{9,8},{10,11... | collective-permute-start | bytes 1572872 | tf_op jit(solution)/shard_map/ppermute | solution.py:175
  70.1 1.5 %collective-permute-done.16.got = bf16[64,4096]{1,0:T(8,128)(2,1)S(1)} collective-permute-done((bf16[64,4096]{1,0:T(8,128)(2,1)S(1)}, bf16[64,4096]{1,0:T(8,128)(2,1)S(1)}, u32[]{:S(2)}, u32[]{:S(2)}) %collective-permute-start.16) | collective-permute-done | bytes 524320 | tf_op jit(solution)/shard_map/ppermute | solution.py:175
  71.7 0.8 %shard_map.95 = bf16[64,8192]{1,0:T(8,128)(2,1)} custom-call(s32[1]{0:T(128)} %bitcast.c_ref, bf16[64,4096]{1,0:T(8,128)(2,1)S(1)} %collective-permute-done.16.got, bf16[64,8192]{1,0:T(8,128)(2,1)} %get-tuple-element.26.whole), custom_call_target="tpu_custom_call", output_to_operand_aliasing={{}: (2, {})} | custom-call | tf_op jit(solution)/shard_map/pallas_call | solution.py:146
  (53 shorter events, 5.6 us)
Async XLA Ops:
  0.0 31.7 %copy-start = (bf16[64,8192]{1,0:T(8,128)(2,1)S(1)}, bf16[64,8192]{1,0:T(8,128)(2,1)}, u32[]{:S(2)}) copy-start(bf16[64,8192]{1,0:T(8,128)(2,1)} %refs_0_.7) | copy-start | bytes 3145732
  3.7 9.8 %collective-permute-start.1 = (bf16[192,512]{1,0:T(8,128)(2,1)S(1)}, bf16[192,512]{1,0:T(8,128)(2,1)S(1)}, u32[]{:S(2)}, u32[]{:S(2)}) collective-permute-start(bf16[192,512]{1,0:T(8,128)(2,1)S(1)} %get-tuple-element.30.refs_4_), channel_id=1, source_target_pairs={{0,4},{1,5},{2,0},{3,1},{4,8},{5,9},{6,2},{7,3},{8,12},{9,13},{10,... | collective-permute-start | bytes 589832 | tf_op jit(solution)/shard_map/ppermute | solution.py:175
  5.8 8.1 %collective-permute-start.12 = (bf16[192,512]{1,0:T(8,128)(2,1)S(1)}, bf16[192,512]{1,0:T(8,128)(2,1)S(1)}, u32[]{:S(2)}, u32[]{:S(2)}) collective-permute-start(bf16[192,512]{1,0:T(8,128)(2,1)S(1)} %get-tuple-element.30.refs_4_), channel_id=1, source_target_pairs={{0,2},{1,3},{2,6},{3,7},{4,0},{5,1},{6,10},{7,11},{8,4},{9,5},{10,... | collective-permute-start | bytes 589832 | tf_op jit(solution)/shard_map/ppermute | solution.py:175
  5.8 13.2 %collective-permute-start.15 = (bf16[192,512]{1,0:T(8,128)(2,1)S(1)}, bf16[192,512]{1,0:T(8,128)(2,1)S(1)}, u32[]{:S(2)}, u32[]{:S(2)}) collective-permute-start(bf16[192,512]{1,0:T(8,128)(2,1)S(1)} %get-tuple-element.29), channel_id=1, source_target_pairs={{0,1},{1,0},{2,3},{3,2},{4,5},{5,4},{6,7},{7,6},{8,9},{9,8},{10,11... | collective-permute-start | bytes 589832 | tf_op jit(solution)/shard_map/ppermute | solution.py:175
  6.8 9.9 %collective-permute-start.5 = (bf16[192,512]{1,0:T(8,128)(2,1)S(1)}, bf16[192,512]{1,0:T(8,128)(2,1)S(1)}, u32[]{:S(2)}, u32[]{:S(2)}) collective-permute-start(bf16[192,512]{1,0:T(8,128)(2,1)S(1)} %get-tuple-element.29), channel_id=1, source_target_pairs={{0,3},{1,2},{2,7},{3,6},{4,1},{5,0},{6,11},{7,10},{8,5},{9,4},{10,... | collective-permute-start | bytes 589832 | tf_op jit(solution)/shard_map/ppermute | solution.py:175
  8.4 9.4 %collective-permute-start.9 = (bf16[192,512]{1,0:T(8,128)(2,1)S(1)}, bf16[192,512]{1,0:T(8,128)(2,1)}, u32[]{:S(2)}, u32[]{:S(2)}) collective-permute-start(bf16[192,512]{1,0:T(8,128)(2,1)S(1)} %get-tuple-element.29), channel_id=1, source_target_pairs={{0,5},{1,4},{2,1},{3,0},{4,9},{5,8},{6,3},{7,2},{8,13},{9,12},{10,... | collective-permute-start | bytes 589832 | tf_op jit(solution)/shard_map/ppermute | solution.py:175
  13.5 18.2 %collective-permute-start = (bf16[64,4096]{1,0:T(8,128)(2,1)}, bf16[64,4096]{1,0:T(8,128)(2,1)S(1)}, u32[]{:S(2)}, u32[]{:S(2)}) collective-permute-start(bf16[64,4096]{1,0:T(8,128)(2,1)} %constant_dynamic-slice_fusion.3), channel_id=1, source_target_pairs={{0,1},{1,0},{2,3},{3,2},{4,5},{5,4},{6,7},{7,6},{8,9},{9,8},{10,11... | collective-permute-start | bytes 1572872 | tf_op jit(solution)/shard_map/ppermute | solution.py:175
  13.9 6.7 %collective-permute-start.2 = (bf16[192,512]{1,0:T(8,128)(2,1)S(1)}, bf16[192,512]{1,0:T(8,128)(2,1)S(1)}, u32[]{:S(2)}, u32[]{:S(2)}) collective-permute-start(bf16[192,512]{1,0:T(8,128)(2,1)S(1)} %collective-permute-done.1.refs_6_), channel_id=1, source_target_pairs={{0,4},{1,5},{2,0},{3,1},{4,8},{5,9},{6,2},{7,3},{8,12},{9,13},{10,... | collective-permute-start | bytes 589832 | tf_op jit(solution)/shard_map/ppermute | solution.py:175
  15.4 0.7 copy-start.1
  16.7 6.3 %collective-permute-start.6 = (bf16[192,512]{1,0:T(8,128)(2,1)S(1)}, bf16[192,512]{1,0:T(8,128)(2,1)S(1)}, u32[]{:S(2)}, u32[]{:S(2)}) collective-permute-start(bf16[192,512]{1,0:T(8,128)(2,1)S(1)} %collective-permute-done.5.refs_9_), channel_id=1, source_target_pairs={{0,2},{1,3},{2,6},{3,7},{4,0},{5,1},{6,10},{7,11},{8,4},{9,5},{10,... | collective-permute-start | bytes 589832 | tf_op jit(solution)/shard_map/ppermute | solution.py:175
  16.9 0.7 copy-start.7
  17.8 6.6 %collective-permute-start.10 = (bf16[192,512]{1,0:T(8,128)(2,1)}, bf16[192,512]{1,0:T(8,128)(2,1)S(1)}, u32[]{:S(2)}, u32[]{:S(2)}) collective-permute-start(bf16[192,512]{1,0:T(8,128)(2,1)} %collective-permute-done.9.refs_7_), channel_id=1, source_target_pairs={{0,4},{1,5},{2,0},{3,1},{4,8},{5,9},{6,2},{7,3},{8,12},{9,13},{10,... | collective-permute-start | bytes 589832 | tf_op jit(solution)/shard_map/ppermute | solution.py:175
  19.1 0.7 copy-start.5
  19.7 7.4 %collective-permute-start.13 = (bf16[192,512]{1,0:T(8,128)(2,1)S(1)}, bf16[192,512]{1,0:T(8,128)(2,1)S(1)}, u32[]{:S(2)}, u32[]{:S(2)}) collective-permute-start(bf16[192,512]{1,0:T(8,128)(2,1)S(1)} %collective-permute-done.12.refs_8_), channel_id=1, source_target_pairs={{0,2},{1,3},{2,6},{3,7},{4,0},{5,1},{6,10},{7,11},{8,4},{9,5},{10,... | collective-permute-start | bytes 589832 | tf_op jit(solution)/shard_map/ppermute | solution.py:175
  20.0 0.7 copy-start.3
  20.6 7.9 %collective-permute-start.3 = (bf16[192,512]{1,0:T(8,128)(2,1)S(1)}, bf16[192,512]{1,0:T(8,128)(2,1)S(1)}, u32[]{:S(2)}, u32[]{:S(2)}) collective-permute-start(bf16[192,512]{1,0:T(8,128)(2,1)S(1)} %collective-permute-done.2.refs_4_), channel_id=1, source_target_pairs={{0,4},{1,5},{2,0},{3,1},{4,8},{5,9},{6,2},{7,3},{8,12},{9,13},{10,... | collective-permute-start | bytes 589832 | tf_op jit(solution)/shard_map/ppermute | solution.py:175
  23.0 8.4 %collective-permute-start.7 = (bf16[192,512]{1,0:T(8,128)(2,1)S(1)}, bf16[192,512]{1,0:T(8,128)(2,1)S(1)}, u32[]{:S(2)}, u32[]{:S(2)}) collective-permute-start(bf16[192,512]{1,0:T(8,128)(2,1)S(1)} %collective-permute-done.6.refs_7_), channel_id=1, source_target_pairs={{0,2},{1,3},{2,6},{3,7},{4,0},{5,1},{6,10},{7,11},{8,4},{9,5},{10,... | collective-permute-start | bytes 589832 | tf_op jit(solution)/shard_map/ppermute | solution.py:175
  24.4 24.8 %collective-permute-start.11 = (bf16[192,512]{1,0:T(8,128)(2,1)S(1)}, bf16[192,512]{1,0:T(8,128)(2,1)S(1)}, u32[]{:S(2)}, u32[]{:S(2)}) collective-permute-start(bf16[192,512]{1,0:T(8,128)(2,1)S(1)} %collective-permute-done.10.refs_5_), channel_id=1, source_target_pairs={{0,4},{1,5},{2,0},{3,1},{4,8},{5,9},{6,2},{7,3},{8,12},{9,13},{10,... | collective-permute-start | bytes 589832 | tf_op jit(solution)/shard_map/ppermute | solution.py:175
  27.2 22.0 %collective-permute-start.14 = (bf16[192,512]{1,0:T(8,128)(2,1)S(1)}, bf16[192,512]{1,0:T(8,128)(2,1)S(1)}, u32[]{:S(2)}, u32[]{:S(2)}) collective-permute-start(bf16[192,512]{1,0:T(8,128)(2,1)S(1)} %collective-permute-done.13.refs_6_), channel_id=1, source_target_pairs={{0,2},{1,3},{2,6},{3,7},{4,0},{5,1},{6,10},{7,11},{8,4},{9,5},{10,... | collective-permute-start | bytes 589832 | tf_op jit(solution)/shard_map/ppermute | solution.py:175
  28.6 27.5 %collective-permute-start.4 = (bf16[192,512]{1,0:T(8,128)(2,1)S(1)}, bf16[192,512]{1,0:T(8,128)(2,1)S(1)}, u32[]{:S(2)}, u32[]{:S(2)}) collective-permute-start(bf16[192,512]{1,0:T(8,128)(2,1)S(1)} %collective-permute-done.3.refs_4_), channel_id=1, source_target_pairs={{0,4},{1,5},{2,0},{3,1},{4,8},{5,9},{6,2},{7,3},{8,12},{9,13},{10,... | collective-permute-start | bytes 589832 | tf_op jit(solution)/shard_map/ppermute | solution.py:175
  31.4 24.7 %collective-permute-start.8 = (bf16[192,512]{1,0:T(8,128)(2,1)S(1)}, bf16[192,512]{1,0:T(8,128)(2,1)S(1)}, u32[]{:S(2)}, u32[]{:S(2)}) collective-permute-start(bf16[192,512]{1,0:T(8,128)(2,1)S(1)} %collective-permute-done.7.refs_7_), channel_id=1, source_target_pairs={{0,2},{1,3},{2,6},{3,7},{4,0},{5,1},{6,10},{7,11},{8,4},{9,5},{10,... | collective-permute-start | bytes 589832 | tf_op jit(solution)/shard_map/ppermute | solution.py:175
  31.7 0.9 %copy-start.2 = (bf16[192,512]{1,0:T(8,128)(2,1)S(1)}, bf16[192,512]{1,0:T(8,128)(2,1)}, u32[]{:S(2)}) copy-start(bf16[192,512]{1,0:T(8,128)(2,1)} %copy-done.1) | copy-start | bytes 589828
  32.6 0.9 %copy-start.4 = (bf16[192,512]{1,0:T(8,128)(2,1)S(1)}, bf16[192,512]{1,0:T(8,128)(2,1)}, u32[]{:S(2)}) copy-start(bf16[192,512]{1,0:T(8,128)(2,1)} %copy-done.3) | copy-start | bytes 589828
  33.5 0.9 %copy-start.6 = (bf16[192,512]{1,0:T(8,128)(2,1)S(1)}, bf16[192,512]{1,0:T(8,128)(2,1)}, u32[]{:S(2)}) copy-start(bf16[192,512]{1,0:T(8,128)(2,1)} %copy-done.5) | copy-start | bytes 589828
  34.5 0.9 %copy-start.8 = (bf16[192,512]{1,0:T(8,128)(2,1)S(1)}, bf16[192,512]{1,0:T(8,128)(2,1)}, u32[]{:S(2)}) copy-start(bf16[192,512]{1,0:T(8,128)(2,1)} %copy-done.7) | copy-start | bytes 589828
  68.4 3.3 %collective-permute-start.16 = (bf16[64,4096]{1,0:T(8,128)(2,1)S(1)}, bf16[64,4096]{1,0:T(8,128)(2,1)S(1)}, u32[]{:S(2)}, u32[]{:S(2)}) collective-permute-start(bf16[64,4096]{1,0:T(8,128)(2,1)S(1)} %get-tuple-element.25), channel_id=1, source_target_pairs={{0,1},{1,0},{2,3},{3,2},{4,5},{5,4},{6,7},{7,6},{8,9},{9,8},{10,11... | collective-permute-start | bytes 1572872 | tf_op jit(solution)/shard_map/ppermute | solution.py:175
